TPU v7x, 128 devices: a whole 4x4x4 slice. The times are simulated.
128 devices in a mesh: req: 32 (over x, z, core), mlp: 4 (over y).
Axes of the slice: x: 4, y: 4, z: 4, core: 2. Of those that a mesh axis runs over, the one named last changes fastest.
Arguments:
- tokens: bfloat16 [4096, 3584], P('req'), may hold values from -40 to 40
- segment_ids: int32 [32, 128], P('req'), may hold values from 0 to 3, never falling along the last dimension, each value on 1 to 64 neighbouring positions
- past_len: int32 [32, 4], P('req'), may hold values from 0 to 2047
- page_table: int32 [32, 64], P('req'), may hold values from 0 to 63, each once within a row
- migrate_pages: int32 [32, 32, 1], P('req'), may hold values from 0 to 31
- pooled_key_cache: bfloat16 [1024, 64, 1024], P('req', None, 'mlp'), may hold values from -6 to 6
- pooled_value_cache: bfloat16 [1024, 64, 1024], P('req', None, 'mlp'), may hold values from -6 to 6
- attn_gain: float32 [3584], replicated, may hold values from 0.25 to 1.75
- w_query: bfloat16 [3584, 2048], P(None, 'mlp'), may hold values from -0.09375 to 0.09375
- key_matrix: bfloat16 [3584, 1024], P(None, 'mlp'), may hold values from -0.09375 to 0.09375
- value_matrix: bfloat16 [3584, 1024], P(None, 'mlp'), may hold values from -0.09375 to 0.09375
- w_out: bfloat16 [2048, 3584], P('mlp'), may hold values from -1 to 1
- post_attn_gain: float32 [3584], replicated, may hold values from 0.25 to 1.75
- ffw_gain: float32 [3584], replicated, may hold values from 0.25 to 1.75
- w_gate: bfloat16 [3584, 14336], P(None, 'req'), may hold values from -0.09375 to 0.09375
- w_up: bfloat16 [3584, 14336], P(None, 'req'), may hold values from -0.09375 to 0.09375
- w_down: bfloat16 [14336, 3584], P('req'), may hold values from -1 to 1
- post_ffw_gain: float32 [3584], replicated, may hold values from 0.25 to 1.75
Outputs:
- mixed: bfloat16 [4096, 3584], P(('req', 'mlp'))
- written_key_rows: bfloat16 [4096, 1024], P('req', 'mlp')
- written_value_rows: bfloat16 [4096, 1024], P('req', 'mlp')
Inputs may be any that keep to these rules, and one draw needn't show every extreme that they name: `segment_ids`: in each row the requests 0 to 3 appear in order; each request has 1 to 64 new tokens, and some request exactly 64. `page_table`: each row is a permutation; every page of the owner's list (own pool and received pages) lies in exactly one request's window. `migrate_pages`: entry [s, d, m] names a page of owner s's pool.
All inputs are finite; a program needn't handle non-finite values.
Results may differ from a plain program's by a relative error of at most 0.015.
Values may be sent and summed in bfloat16 or wider, within the bound.
No kernel may reach another device: no remote copies, remote signals or barrier semaphores. Data moves between devices by JAX's collectives and lax.ppermute only.
A program may use at most 128 MiB of HBM per device.

v0:
```python
import jax
import jax.numpy as jnp
from jax import lax
from jax.sharding import PartitionSpec as P

HEAD_SIZE = 256
WINDOW_LENGTH = 1024
SOFT_CAP = 50.0
NORM_EPS = 1e-06
ROPE_BASE = 10000.0


def rms_scale(values, gain):
    return values * lax.rsqrt(jnp.mean(values * values, axis=-1, keepdims=True) + NORM_EPS) * gain


def apply_rotary(vectors, token_positions):
    width = vectors.shape[-1]
    half = width // 2
    frequency = ROPE_BASE ** (-jnp.arange(half, dtype=jnp.float32) * (2.0 / width))
    angles = token_positions.astype(jnp.float32)[:, None] * frequency[None, :]
    cosine = jnp.cos(angles)[:, None, :]
    sine = jnp.sin(angles)[:, None, :]
    first = vectors[..., :half]
    second = vectors[..., half:]
    return jnp.concatenate(
        [first * cosine - second * sine, second * cosine + first * sine], axis=-1
    )


def token_layout(segment, past):
    requests = jnp.arange(past.shape[0], dtype=jnp.int32)
    member = segment[:, None] == requests[None, :]
    firsts = jnp.sum((segment[:, None] < requests[None, :]).astype(jnp.int32), axis=0)
    offsets = jnp.arange(segment.shape[0], dtype=jnp.int32) - jnp.sum(
        jnp.where(member, firsts[None, :], 0), axis=1
    )
    token_positions = jnp.sum(jnp.where(member, past[None, :], 0), axis=1) + offsets
    return (offsets, token_positions)


def visibility(segment, offsets, past, window):
    count_req = past.shape[0]
    requests = jnp.arange(count_req, dtype=jnp.int32)
    slots = jnp.arange(count_req * window, dtype=jnp.int32)
    slot_req = slots // window
    slot_pos = slots % window
    slot_past = jnp.sum(jnp.where(slot_req[:, None] == requests[None, :], past[None, :], 0), axis=1)
    cached = (
        (segment[:, None] == slot_req[None, :])
        & (slot_pos[None, :] > offsets[:, None])
        & (slot_pos[None, :] >= window - slot_past[None, :])
    )
    order = jnp.arange(segment.shape[0], dtype=jnp.int32)
    fresh = (segment[:, None] == segment[None, :]) & (order[None, :] <= order[:, None])
    return (cached, fresh)


def local(
    tokens,
    segment_ids,
    past_len,
    page_table,
    migrate_pages,
    pooled_key_cache,
    pooled_value_cache,
    attn_gain,
    w_query,
    key_matrix,
    value_matrix,
    w_out,
    post_attn_gain,
    ffw_gain,
    w_gate,
    w_up,
    w_down,
    post_ffw_gain,
):
    tok_count = tokens.shape[0]
    key_heads = key_matrix.shape[1] // HEAD_SIZE
    query_heads = w_query.shape[1] // HEAD_SIZE
    query_group = query_heads // key_heads
    scale = float(HEAD_SIZE) ** (-0.5)
    page_len = pooled_key_cache.shape[1]
    columns = pooled_key_cache.shape[2]
    send_list = migrate_pages[0]
    owners = send_list.shape[0]
    flat_list = send_list.reshape(-1)
    send_keys = jnp.take(pooled_key_cache, flat_list, axis=0).reshape(
        owners, send_list.shape[1], page_len, columns
    )
    send_values = jnp.take(pooled_value_cache, flat_list, axis=0).reshape(
        owners, send_list.shape[1], page_len, columns
    )
    recv_keys, recv_values = (
        lax.all_to_all(send_keys, "req", split_axis=0, concat_axis=0, tiled=True),
        lax.all_to_all(send_values, "req", split_axis=0, concat_axis=0, tiled=True),
    )
    page_lookup = page_table[0]
    listed_keys = jnp.concatenate(
        [pooled_key_cache, recv_keys.reshape(-1, page_len, columns)], axis=0
    )
    listed_values = jnp.concatenate(
        [pooled_value_cache, recv_values.reshape(-1, page_len, columns)], axis=0
    )
    window_keys = jnp.take(listed_keys, page_lookup, axis=0).reshape(-1, key_heads, HEAD_SIZE)
    window_values = jnp.take(listed_values, page_lookup, axis=0).reshape(-1, key_heads, HEAD_SIZE)
    segment = segment_ids[0]
    past = past_len[0]
    offsets, token_positions = token_layout(segment, past)
    normalized_input = rms_scale(tokens.astype(jnp.float32), attn_gain).astype(jnp.bfloat16)
    query_rows = apply_rotary(
        jnp.dot(normalized_input, w_query, preferred_element_type=jnp.float32).reshape(
            tok_count, query_heads, HEAD_SIZE
        ),
        token_positions,
    ).astype(jnp.bfloat16)
    incoming_keys = apply_rotary(
        jnp.dot(normalized_input, key_matrix, preferred_element_type=jnp.float32).reshape(
            tok_count, key_heads, HEAD_SIZE
        ),
        token_positions,
    ).astype(jnp.bfloat16)
    incoming_values = jnp.dot(
        normalized_input, value_matrix, preferred_element_type=jnp.float32
    ).astype(jnp.bfloat16)
    grouped_queries = query_rows.reshape(tok_count, key_heads, query_group, HEAD_SIZE)
    value_heads = incoming_values.reshape(tok_count, key_heads, HEAD_SIZE)
    score_cached = jnp.einsum(
        "tkgd,skd->tkgs", grouped_queries, window_keys, preferred_element_type=jnp.float32
    )
    score_fresh = jnp.einsum(
        "tkgd,skd->tkgs", grouped_queries, incoming_keys, preferred_element_type=jnp.float32
    )
    cached, fresh = visibility(segment, offsets, past, WINDOW_LENGTH)
    weight_cached = jnp.where(
        cached[:, None, None, :],
        jnp.exp(SOFT_CAP * jnp.tanh(score_cached * (scale / SOFT_CAP))),
        0.0,
    )
    weight_fresh = jnp.where(
        fresh[:, None, None, :], jnp.exp(SOFT_CAP * jnp.tanh(score_fresh * (scale / SOFT_CAP))), 0.0
    )
    totals = jnp.sum(weight_cached, axis=-1, keepdims=True) + jnp.sum(
        weight_fresh, axis=-1, keepdims=True
    )
    prob_cached = (weight_cached / totals).astype(jnp.bfloat16)
    prob_fresh = (weight_fresh / totals).astype(jnp.bfloat16)
    attended = jnp.einsum(
        "tkgs,skd->tkgd", prob_cached, window_values, preferred_element_type=jnp.float32
    )
    attended = attended + jnp.einsum(
        "tkgs,skd->tkgd", prob_fresh, value_heads, preferred_element_type=jnp.float32
    )
    attention = attended.astype(jnp.bfloat16).reshape(tok_count, query_heads * HEAD_SIZE)
    rows_mine = tok_count // lax.axis_size("mlp")
    attn_out = lax.psum_scatter(
        jnp.dot(attention, w_out, preferred_element_type=jnp.float32).astype(jnp.bfloat16),
        "mlp",
        scatter_dimension=0,
        tiled=True,
    ).astype(jnp.float32)
    own_rows = lax.dynamic_slice_in_dim(
        tokens, lax.axis_index("mlp") * rows_mine, rows_mine, 0
    ).astype(jnp.float32)
    residual_stream = own_rows + rms_scale(attn_out, post_attn_gain)
    feedforward_input = rms_scale(residual_stream, ffw_gain).astype(jnp.bfloat16)
    piece = lax.all_gather(feedforward_input, "req", axis=0, tiled=True)
    gate_part = jnp.dot(piece, w_gate, preferred_element_type=jnp.float32)
    up_part = jnp.dot(piece, w_up, preferred_element_type=jnp.float32)
    hidden = (jax.nn.gelu(gate_part, approximate=True) * up_part).astype(jnp.bfloat16)
    ffw_out = lax.psum_scatter(
        jnp.dot(hidden, w_down, preferred_element_type=jnp.float32).astype(jnp.bfloat16),
        "req",
        scatter_dimension=0,
        tiled=True,
    ).astype(jnp.float32)
    mixed = (residual_stream + rms_scale(ffw_out, post_ffw_gain)).astype(jnp.bfloat16)
    return (mixed, incoming_keys.reshape(tok_count, key_heads * HEAD_SIZE), incoming_values)


def solution(mesh):
    return jax.shard_map(
        local,
        mesh=mesh,
        in_specs=(
            P("req", None),
            P("req", None),
            P("req", None),
            P("req", None),
            P("req", None, None),
            P("req", None, "mlp"),
            P("req", None, "mlp"),
            P(),
            P(None, "mlp"),
            P(None, "mlp"),
            P(None, "mlp"),
            P("mlp", None),
            P(),
            P(),
            P(None, "req"),
            P(None, "req"),
            P("req", None),
            P(),
        ),
        out_specs=(P(("req", "mlp"), None), P("req", "mlp"), P("req", "mlp")),
        check_vma=False,
    )
```

profile of v0, /device:TPU:0, one launch (start us, length us, event | category | flops | bytes accessed | tf_op | source)
XLA Modules:
  0.0 282.2 jit_solution(7771821692837029242)
XLA Ops:
  7.2 0.0 copy-start
  7.2 0.8 compare_and_fusion.1
  8.0 0.8 compare_select_fusion.1
  8.8 2.8 gather_fusion.2
  11.6 2.9 %gather_fusion = bf16[32,64,256]{2,1,0:T(8,128)(2,1)} fusion(bf16[32,64,256]{2,1,0:T(8,128)(2,1)} %param.28, s32[1024]{0:T(1024)S(1)} %pad_clamp_fusion.1), kind=kCustom, calls=%fused_computation.clone | custom fusion | bytes 2097280 | tf_op jit(solution)/shard_map/jit(_take)/gather | solution.py:92
  14.5 3.1 %select_bitcast_fusion = (bf16[32,1,64,256]{3,2,1,0:T(8,128)(2,1)}, bf16[32,1,64,256]{3,2,1,0:T(8,128)(2,1)}) fusion(bf16[32,64,256]{2,1,0:T(8,128)(2,1)} %gather_fusion.2, pred[32]{0:T(512)(128)(4,1)S(1)} %compare_and_fusion.1, bf16[32,64,256]{2,1,0:T(8,128)(2,1)} %gather_fusion), kind=kLoop, calls=%fused_computation.45 | loop fusion | flops 1048576 | bytes 4194336 | tf_op jit(solution)/shard_map/reshape | solution.py:89
  17.6 8.5 %all-to-all-start = ((bf16[32,1,64,256]{3,2,1,0:T(8,128)(2,1)}), bf16[32,1,64,256]{3,2,1,0:T(8,128)(2,1)}, u32[]{:S(2)}, u32[]{:S(2)}) async-start(bf16[32,1,64,256]{3,2,1,0:T(8,128)(2,1)} %get-tuple-element.20), calls=%async_computation | async-start | bytes 2097152 | tf_op jit(solution)/shard_map/all_to_all | solution.py:97
  26.2 0.6 compare_and_fusion
  26.8 0.6 fusion.44
  27.4 1.7 fusion.7
  29.1 0.7 fusion.43
  29.8 0.1 select_reduce_fusion.1
  30.0 0.1 select_reduce_fusion.2
  30.0 0.1 select_reduce_fusion
  30.2 0.6 subtract_compare_fusion
  30.8 0.6 add_convert_fusion.1
  31.3 0.9 multiply_cosine_fusion.1
  32.3 0.0 copy-done.16
  32.3 2.2 convolution_bitcast_fusion
  34.5 0.3 fusion.49
  34.9 1.4 fusion.57
  36.3 0.6 pad_maximum_fusion.5
  36.9 0.6 pad_clamp_fusion
  37.5 1.1 reshape.421
  38.6 0.1 fusion.59
  38.7 0.9 subtract_convert_fusion
  39.6 1.7 fusion.61
  41.4 2.3 convolution_convert_fusion.2
  43.6 0.0 copy-start.18
  43.7 0.0 all-to-all-done
  43.7 7.4 %all-to-all-start.1 = ((bf16[32,1,64,256]{3,2,1,0:T(8,128)(2,1)}), bf16[32,1,64,256]{3,2,1,0:T(8,128)(2,1)}, u32[]{:S(2)}, u32[]{:S(2)}) async-start(bf16[32,1,64,256]{3,2,1,0:T(8,128)(2,1)} %get-tuple-element.19), calls=%async_computation.1 | async-start | bytes 2097152 | tf_op jit(solution)/shard_map/all_to_all | solution.py:96
  51.1 0.0 reduce-scatter.3.cloned.1.call-start
  51.2 4.6 %and_and_fusion = pred[128,4096]{0,1:T(8,128)(4,1)} fusion(s32[128]{0:T(128)S(1)} %copy-done.13, s32[128]{0:T(128)S(1)} %bitcast.86, s32[4096]{0:T(1024)S(1)} %copy-done.6, s32[4096]{0:T(1024)S(1)} %get-tuple-element.26, pred[4096]{0:T(1024)(128)(4,1)S(1)} %copy-done.8), kind=kLoop, calls=%fused_computation.22 | loop fusion | flops 2097152 | bytes 562176 | tf_op jit(solution)/shard_map/and | solution.py:50
  55.8 3.0 %pad_maximum_fusion = bf16[64,64,256]{2,1,0:T(8,128)(2,1)} fusion(bf16[32,64,256]{2,1,0:T(8,128)(2,1)} %bitcast.3, bf16[32,64,256]{2,1,0:T(8,128)(2,1)} %param.28), kind=kLoop, calls=%fused_computation.16 | loop fusion | flops 1048576 | bytes 4194304 | tf_op jit(solution)/shard_map/concatenate | solution.py:103
  58.9 9.0 %all-to-all-done.1 = bf16[32,1,64,256]{3,2,1,0:T(8,128)(2,1)} async-done(((bf16[32,1,64,256]{3,2,1,0:T(8,128)(2,1)}), bf16[32,1,64,256]{3,2,1,0:T(8,128)(2,1)}, u32[]{:S(2)}, u32[]{:S(2)}) %all-to-all-start.1) | async-done | bytes 1048608 | tf_op jit(solution)/shard_map/all_to_all | solution.py:96
  67.9 3.1 %pad_maximum_fusion.1 = bf16[64,64,256]{2,1,0:T(8,128)(2,1)} fusion(bf16[32,64,256]{2,1,0:T(8,128)(2,1)} %bitcast.9, bf16[32,64,256]{2,1,0:T(8,128)(2,1)} %param.27), kind=kLoop, calls=%fused_computation.17 | loop fusion | flops 1048576 | bytes 4194304 | tf_op jit(solution)/shard_map/concatenate | solution.py:100
  71.0 3.7 %gather_fusion.1 = bf16[64,64,256]{2,1,0:T(8,128)(2,1)} fusion(bf16[64,64,256]{2,1,0:T(8,128)(2,1)} %pad_maximum_fusion, s32[1024]{0:T(1024)} %pad_clamp_fusion), kind=kCustom, calls=%fused_computation.1.clone | custom fusion | bytes 4194560 | tf_op jit(solution)/shard_map/jit(_take)/gather | solution.py:107
  74.7 3.7 %gather_fusion.3 = bf16[64,64,256]{2,1,0:T(8,128)(2,1)} fusion(bf16[64,64,256]{2,1,0:T(8,128)(2,1)} %pad_maximum_fusion.1, s32[1024]{0:T(1024)} %pad_clamp_fusion), kind=kCustom, calls=%fused_computation.3.clone | custom fusion | bytes 4194560 | tf_op jit(solution)/shard_map/jit(_take)/gather | solution.py:106
  78.4 0.0 copy-done.14
  78.4 2.7 broadcast_select_fusion
  81.1 1.4 fusion.60
  82.5 0.0 copy-start.19
  82.5 0.0 copy-start.1
  82.5 0.8 fusion.5
  83.3 0.1 copy-done.19
  83.4 0.2 fusion.19
  83.6 1.0 copy-done.1
  84.6 1.6 convolution_convert_fusion.1
  86.2 0.0 reduce-scatter.3.cloned.1.call-update
  86.3 0.0 all-gather.2.cloned.1.call-start
  86.3 21.4 %reduce-scatter.3.cloned.1.call-done = bf16[32,3584]{1,0:T(8,128)(2,1)} async-done(((bf16[128,3584]{1,0:T(8,128)(2,1)}), bf16[32,3584]{1,0:T(8,128)(2,1)}) %reduce-scatter.3.cloned.1.call-update) | async-done | bytes 229392 | tf_op jit(solution)/shard_map/reduce_scatter | solution.py:157
  107.7 1.1 fusion.25
  108.8 1.3 multiply_reduce_fusion
  110.2 1.9 multiply_convert_fusion
  112.1 0.0 all-gather.2.cloned.1.call-update
  112.1 0.2 reduce-scatter.5.cloned.1.call-start
  112.4 50.6 %all-gather.2.cloned.1.call-done = bf16[1024,3584]{1,0:T(8,128)(2,1)} async-done(((bf16[32,3584]{1,0:T(8,128)(2,1)}), bf16[1024,3584]{1,0:T(8,128)(2,1)}) %all-gather.2.cloned.1.call-update) | async-done | bytes 7340048 | tf_op jit(solution)/shard_map/all_gather | solution.py:168
  162.9 8.7 %fusion.62 = f32[1024,448]{0,1:T(8,128)} fusion(bf16[1024,3584]{1,0:T(8,128)(2,1)} %all-gather.2.cloned.1.call-done, bf16[3584,448]{0,1:T(8,128)(2,1)} %param.36), kind=kOutput, calls=%fused_computation.122 | convolution fusion | flops 3288334336 | bytes 12386304 | tf_op jit(solution)/shard_map/dot_general | solution.py:169
  171.7 0.0 copy-done
  171.7 13.0 %convolution_convert_fusion = bf16[1024,3584]{1,0:T(8,128)(2,1)} fusion(bf16[448,3584]{1,0:T(8,128)(2,1)S(1)} %copy-done, f32[1024,448]{0,1:T(8,128)} %fusion.62, bf16[1024,3584]{1,0:T(8,128)(2,1)} %all-gather.2.cloned.1.call-done, bf16[3584,448]{0,1:T(8,128)(2,1)} %param.37), kind=kOutput, calls=%fused_computation.4 | convolution fusion | flops 6584926208 | bytes 22937600 | tf_op jit(solution)/shard_map/dot_general | solution.py:173
  184.7 0.0 reduce-scatter.5.cloned.1.call-update
  184.8 87.8 %reduce-scatter.5.cloned.1.call-done = bf16[32,3584]{1,0:T(8,128)(2,1)} async-done(((bf16[1024,3584]{1,0:T(8,128)(2,1)}), bf16[32,3584]{1,0:T(8,128)(2,1)}) %reduce-scatter.5.cloned.1.call-update) | async-done | bytes 229392 | tf_op jit(solution)/shard_map/reduce_scatter | solution.py:172
  272.6 1.1 fusion.28
  273.7 2.0 fusion.31
  (41 shorter events, 0.1 us)
Async XLA Ops:
  7.2 164.5 %copy-start = (bf16[448,3584]{1,0:T(8,128)(2,1)S(1)}, bf16[448,3584]{1,0:T(8,128)(2,1)}, u32[]{:S(2)}) copy-start(bf16[448,3584]{1,0:T(8,128)(2,1)} %param.38) | copy-start | bytes 9633796
  17.6 8.6 %copy-start.17 = (s32[1,64]{1,0:T(1,128)S(1)}, s32[1,64]{1,0:T(1,128)}, u32[]{:S(2)}) copy-start(s32[1,64]{1,0:T(1,128)} %param.25) | copy-start | bytes 772
  17.6 11.5 %copy-start.10 = (s32[1,128]{1,0:T(1,128)S(1)}, s32[1,128]{1,0:T(1,128)}, u32[]{:S(2)}) copy-start(s32[1,128]{1,0:T(1,128)} %param.23) | copy-start | bytes 1540
  17.6 12.2 %copy-start.12 = (s32[1,4]{1,0:T(1,128)S(1)}, s32[1,4]{1,0:T(1,128)}, u32[]{:S(2)}) copy-start(s32[1,4]{1,0:T(1,128)} %param.24) | copy-start | bytes 52
  17.6 14.7 %copy-start.16 = (f32[3584]{0:T(1024)S(1)}, f32[3584]{0:T(1024)}, u32[]{:S(2)}) copy-start(f32[3584]{0:T(1024)} %param.29) | copy-start | bytes 43012
  17.6 26.0 %all-to-all-start = ((bf16[32,1,64,256]{3,2,1,0:T(8,128)(2,1)}), bf16[32,1,64,256]{3,2,1,0:T(8,128)(2,1)}, u32[]{:S(2)}, u32[]{:S(2)}) async-start(bf16[32,1,64,256]{3,2,1,0:T(8,128)(2,1)} %get-tuple-element.20), calls=%async_computation | async-start | bytes 2097152 | tf_op jit(solution)/shard_map/all_to_all | solution.py:97
  26.8 8.1 %copy-start.15 = (bf16[3584,512]{1,0:T(8,128)(2,1)S(1)}, bf16[3584,512]{1,0:T(8,128)(2,1)}, u32[]{:S(2)}) copy-start(bf16[3584,512]{1,0:T(8,128)(2,1)} %param.30) | copy-start | bytes 11010052
  27.4 7.5 %copy-start.3 = (bf16[128,3584]{1,0:T(8,128)(2,1)S(1)}, bf16[128,3584]{1,0:T(8,128)(2,1)}, u32[]{:S(2)}) copy-start(bf16[128,3584]{1,0:T(8,128)(2,1)} %param.22) | copy-start | bytes 2752516
  29.1 7.1 %copy-start.20 = (f32[128]{0:T(128)}, f32[128]{0:T(128)S(1)}, u32[]{:S(2)}) copy-start(f32[128]{0:T(128)S(1)} %add_rsqrt_fusion.3) | copy-start | bytes 1540
  41.4 9.8 %copy-start.6 = (s32[4096]{0:T(1024)S(1)}, s32[4096]{0:T(1024)}, u32[]{:S(2)}) copy-start(s32[4096]{0:T(1024)} %get-tuple-element.25) | copy-start | bytes 49156
  41.4 9.8 %copy-start.8 = (pred[4096]{0:T(1024)(128)(4,1)S(1)}, pred[4096]{0:T(1024)(128)(4,1)}, u32[]{:S(2)}) copy-start(pred[4096]{0:T(1024)(128)(4,1)} %subtract_compare_fusion) | copy-start | bytes 12292
  41.4 9.8 %copy-start.11 = (s32[1,128]{1,0:T(1,128)S(1)}, s32[1,128]{1,0:T(1,128)}, u32[]{:S(2)}) copy-start(s32[1,128]{1,0:T(1,128)} %param.23) | copy-start | bytes 1540
  41.4 9.8 %copy-start.13 = (s32[128]{0:T(128)S(1)}, s32[128]{0:T(128)}, u32[]{:S(2)}) copy-start(s32[128]{0:T(128)} %get-tuple-element.16) | copy-start | bytes 1540
  43.6 39.7 %copy-start.18 = (bf16[128,256]{1,0:T(8,128)(2,1)}, bf16[128,256]{1,0:T(8,128)(2,1)S(1)}, u32[]{:S(2)}) copy-start(bf16[128,256]{1,0:T(8,128)(2,1)S(1)} %convolution_convert_fusion.2) | copy-start | bytes 196612
  43.7 24.2 %all-to-all-start.1 = ((bf16[32,1,64,256]{3,2,1,0:T(8,128)(2,1)}), bf16[32,1,64,256]{3,2,1,0:T(8,128)(2,1)}, u32[]{:S(2)}, u32[]{:S(2)}) async-start(bf16[32,1,64,256]{3,2,1,0:T(8,128)(2,1)} %get-tuple-element.19), calls=%async_computation.1 | async-start | bytes 2097152 | tf_op jit(solution)/shard_map/all_to_all | solution.py:96
  51.1 56.6 %reduce-scatter.3.cloned.1.call-start = ((), (), s32[]{:S(2)}) async-start(), calls=%async_computation.4 | async-start | bytes 1146880 | tf_op jit(solution)/shard_map/reduce_scatter | solution.py:157
  74.7 3.7 %copy-start.14 = (pred[64]{0:T(512)(128)(4,1)S(1)}, pred[64]{0:T(512)(128)(4,1)}, u32[]{:S(2)}) copy-start(pred[64]{0:T(512)(128)(4,1)} %compare_and_fusion) | copy-start | bytes 196
  78.4 2.7 copy-start.4
  82.5 0.9 copy-start.19
  82.5 2.1 copy-start.1
  84.6 24.2 %copy-start.5 = (f32[3584]{0:T(1024)S(1)}, f32[3584]{0:T(1024)}, u32[]{:S(2)}) copy-start(f32[3584]{0:T(1024)} %param.34) | copy-start | bytes 43012
  84.6 25.5 %copy-start.9 = (f32[3584]{0:T(1024)S(1)}, f32[3584]{0:T(1024)}, u32[]{:S(2)}) copy-start(f32[3584]{0:T(1024)} %param.35) | copy-start | bytes 43012
  86.3 76.7 %all-gather.2.cloned.1.call-start = ((), (), s32[]{:S(2)}) async-start(), calls=%async_computation.5 | async-start | bytes 7569408 | tf_op jit(solution)/shard_map/all_gather | solution.py:168
  112.1 160.4 %reduce-scatter.5.cloned.1.call-start = ((), (), s32[]{:S(2)}) async-start(), calls=%async_computation.6 | async-start | bytes 7569408 | tf_op jit(solution)/shard_map/reduce_scatter | solution.py:172
  184.7 89.0 %copy-start.2 = (bf16[32,3584]{1,0:T(8,128)(2,1)S(1)}, bf16[32,3584]{1,0:T(8,128)(2,1)}, u32[]{:S(2)}) copy-start(bf16[32,3584]{1,0:T(8,128)(2,1)} %reduce-scatter.3.cloned.1.call-done) | copy-start | bytes 688132
  184.7 89.0 %copy-start.7 = (f32[3584]{0:T(1024)S(1)}, f32[3584]{0:T(1024)}, u32[]{:S(2)}) copy-start(f32[3584]{0:T(1024)} %param.39) | copy-start | bytes 43012
Sparse Core Ops, SparseCore 0:
  86.4 21.2 reduce-scatter.2
  112.2 50.6 all-gather.1
  184.9 87.6 reduce-scatter.4
where the time goes:
time: 283 us; the launch traced here: 282 us
  waiting for transfers between devices  169 us (60%)
  other arithmetic  34.1 us (12%)
  matrix products  33.4 us (12%)
  starting transfers between devices  16.3 us (6%)
  local copies, waits for them, and re-layouts  15.5 us (5%)
  between operations  14 us (5%)
    reduce_scatter x1, waiting for transfers between devices, local(): lax.psum_scatter(jnp.dot(hidden, w_down, preferred_element_type=jnp.float...  87.8 us
    all_gather x1, waiting for transfers between devices, local(): piece = lax.all_gather(feedforward_input, 'req', axis=0, tiled=True)  50.6 us
    reduce_scatter x1, waiting for transfers between devices, local(): lax.psum_scatter(jnp.dot(attention, w_out, preferred_element_type=jnp.flo...  21.4 us
    dot_general x1, matrix products, local(): jnp.dot(hidden, w_down, preferred_element_type=jnp.float32)  13 us
    all_to_all x1, waiting for transfers between devices, local(): lax.all_to_all(send_keys, 'req', split_axis=0, concat_axis=0, tiled=True)  9.04 us
    dot_general x1, matrix products, local(): gate_part = jnp.dot(piece, w_gate, preferred_element_type=jnp.float32)  8.75 us
    all_to_all x1, starting transfers between devices, local(): lax.all_to_all(send_values, 'req', split_axis=0, concat_axis=0, tiled=True)  8.52 us
    all_to_all x1, starting transfers between devices, local(): lax.all_to_all(send_keys, 'req', split_axis=0, concat_axis=0, tiled=True)  7.45 us
  transfers between devices with their start and end apart: 5, of which 4 were waited for; matrix products, arithmetic and copies ran while one was open for 9% of the time, Pallas kernels for 0%

commit v1 on v0

--- a/solution.py
+++ b/solution.py
@@ -165,7 +165,9 @@
     ).astype(jnp.float32)
     residual_stream = own_rows + rms_scale(attn_out, post_attn_gain)
     feedforward_input = rms_scale(residual_stream, ffw_gain).astype(jnp.bfloat16)
-    piece = lax.all_gather(feedforward_input, "req", axis=0, tiled=True)
+    piece = jnp.concatenate(
+        lax.all_to_all(jnp.stack([feedforward_input] * lax.axis_size("req")), "req", 0, 0), axis=0
+    )
     gate_part = jnp.dot(piece, w_gate, preferred_element_type=jnp.float32)
     up_part = jnp.dot(piece, w_up, preferred_element_type=jnp.float32)
     hidden = (jax.nn.gelu(gate_part, approximate=True) * up_part).astype(jnp.bfloat16)

time: 283 us -> 321 us (1.13)
  blocking collectives: 0 us -> 91.5 us
  waiting for transfers between devices: 169 us -> 116 us
  matrix products: 33.4 us -> 29.4 us
  local copies, waits for them, and re-layouts: 15.5 us -> 19.3 us
    all_to_all x0 -> x1, blocking collectives: none -> 91.5 us  [local(): lax.all_to_all(jnp.stack([feedforward_input] * lax.axis_size('req')), 're...]
    all_gather x1 -> x0, waiting for transfers between devices: 50.6 us -> none  [local(): piece = lax.all_gather(feedforward_input, 'req', axis=0, tiled=True)]
    dot_general x1, matrix products: 8.75 us -> 4.73 us  [local(): gate_part = jnp.dot(piece, w_gate, preferred_element_type=jnp.float32)]
  transfers between devices with their start and end apart: 5 -> 4, of which waited for: 4 -> 3; matrix products, arithmetic and copies ran while one was open for 9% -> 8% of each run, Pallas kernels for 0% -> 0%
where the time goes in v1:
time: 321 us; the launch traced here: 320 us
  waiting for transfers between devices  116 us (36%)
  blocking collectives  91.5 us (29%)
  other arithmetic  33.4 us (10%)
  matrix products  29.4 us (9%)
  local copies, waits for them, and re-layouts  19.3 us (6%)
  starting transfers between devices  16 us (5%)
  between operations  14.4 us (4%)
    all_to_all x1, blocking collectives, local(): lax.all_to_all(jnp.stack([feedforward_input] * lax.axis_size('req')), 're...  91.5 us
    reduce_scatter x1, waiting for transfers between devices, local(): lax.psum_scatter(jnp.dot(hidden, w_down, preferred_element_type=jnp.float...  85.2 us
    reduce_scatter x1, waiting for transfers between devices, local(): lax.psum_scatter(jnp.dot(attention, w_out, preferred_element_type=jnp.flo...  21.4 us
    dot_general x1, matrix products, local(): jnp.dot(hidden, w_down, preferred_element_type=jnp.float32)  13 us
    all_to_all x1, waiting for transfers between devices, local(): lax.all_to_all(send_keys, 'req', split_axis=0, concat_axis=0, tiled=True)  9.02 us
    all_to_all x1, starting transfers between devices, local(): lax.all_to_all(send_values, 'req', split_axis=0, concat_axis=0, tiled=True)  8.52 us
    all_to_all x1, starting transfers between devices, local(): lax.all_to_all(send_keys, 'req', split_axis=0, concat_axis=0, tiled=True)  7.44 us
  transfers between devices with their start and end apart: 4, of which 3 were waited for; matrix products, arithmetic and copies ran while one was open for 8% of the time, Pallas kernels for 0%

profile of v1, /device:TPU:0, one launch (start us, length us, event | category | flops | bytes accessed | tf_op | source)
XLA Modules:
  0.0 319.7 jit_solution(863725572466236379)
XLA Ops:
  7.2 0.0 copy-start
  7.2 0.8 compare_and_fusion.1
  8.0 0.8 compare_select_fusion.1
  8.8 2.8 gather_fusion.2
  11.6 2.9 gather_fusion
  14.5 3.1 select_bitcast_fusion
  17.6 8.5 %all-to-all-start = ((bf16[32,1,64,256]{3,2,1,0:T(8,128)(2,1)}), bf16[32,1,64,256]{3,2,1,0:T(8,128)(2,1)}, u32[]{:S(2)}, u32[]{:S(2)}) async-start(bf16[32,1,64,256]{3,2,1,0:T(8,128)(2,1)} %get-tuple-element.20), calls=%async_computation | async-start | bytes 2097152 | tf_op jit(solution)/shard_map/all_to_all | solution.py:97
  26.2 0.5 compare_and_fusion
  26.7 0.6 fusion.44
  27.3 1.7 fusion.7
  29.1 0.0 copy-done.11
  29.1 0.7 fusion.43
  29.8 0.1 select_reduce_fusion.1
  29.9 0.1 select_reduce_fusion.2
  30.0 0.1 select_reduce_fusion
  30.1 0.6 subtract_compare_fusion
  30.7 0.5 add_convert_fusion.1
  31.3 0.9 multiply_cosine_fusion.1
  32.2 2.2 convolution_bitcast_fusion
  34.5 0.3 fusion.49
  34.8 1.4 fusion.57
  36.2 0.0 copy-done.22
  36.2 0.6 pad_maximum_fusion.5
  36.9 0.6 pad_clamp_fusion
  37.5 1.1 reshape.426
  38.6 0.1 fusion.59
  38.7 0.9 subtract_convert_fusion
  39.6 1.7 fusion.61
  41.3 2.3 convolution_convert_fusion.2
  43.6 0.0 copy-start.20
  43.6 0.0 all-to-all-done
  43.6 7.4 %all-to-all-start.1 = ((bf16[32,1,64,256]{3,2,1,0:T(8,128)(2,1)}), bf16[32,1,64,256]{3,2,1,0:T(8,128)(2,1)}, u32[]{:S(2)}, u32[]{:S(2)}) async-start(bf16[32,1,64,256]{3,2,1,0:T(8,128)(2,1)} %get-tuple-element.19), calls=%async_computation.1 | async-start | bytes 2097152 | tf_op jit(solution)/shard_map/all_to_all | solution.py:96
  51.1 0.0 reduce-scatter.3.cloned.1.call-start
  51.1 4.6 %and_and_fusion = pred[128,4096]{0,1:T(8,128)(4,1)} fusion(s32[128]{0:T(128)S(1)} %copy-done.14, s32[128]{0:T(128)S(1)} %bitcast.89, s32[4096]{0:T(1024)S(1)} %copy-done.7, s32[4096]{0:T(1024)S(1)} %get-tuple-element.26, pred[4096]{0:T(1024)(128)(4,1)S(1)} %copy-done.9), kind=kLoop, calls=%fused_computation.22 | loop fusion | flops 2097152 | bytes 562176 | tf_op jit(solution)/shard_map/and | solution.py:50
  55.8 3.0 pad_maximum_fusion
  58.8 9.0 %all-to-all-done.1 = bf16[32,1,64,256]{3,2,1,0:T(8,128)(2,1)} async-done(((bf16[32,1,64,256]{3,2,1,0:T(8,128)(2,1)}), bf16[32,1,64,256]{3,2,1,0:T(8,128)(2,1)}, u32[]{:S(2)}, u32[]{:S(2)}) %all-to-all-start.1) | async-done | bytes 1048608 | tf_op jit(solution)/shard_map/all_to_all | solution.py:96
  67.8 3.1 pad_maximum_fusion.1
  70.9 3.7 %gather_fusion.1 = bf16[64,64,256]{2,1,0:T(8,128)(2,1)} fusion(bf16[64,64,256]{2,1,0:T(8,128)(2,1)} %pad_maximum_fusion, s32[1024]{0:T(1024)} %pad_clamp_fusion), kind=kCustom, calls=%fused_computation.1.clone | custom fusion | bytes 4194560 | tf_op jit(solution)/shard_map/jit(_take)/gather | solution.py:107
  74.6 3.7 %gather_fusion.3 = bf16[64,64,256]{2,1,0:T(8,128)(2,1)} fusion(bf16[64,64,256]{2,1,0:T(8,128)(2,1)} %pad_maximum_fusion.1, s32[1024]{0:T(1024)} %pad_clamp_fusion), kind=kCustom, calls=%fused_computation.3.clone | custom fusion | bytes 4194560 | tf_op jit(solution)/shard_map/jit(_take)/gather | solution.py:106
  78.3 2.7 broadcast_select_fusion
  81.1 1.4 fusion.60
  82.4 0.0 copy-start.21
  82.4 0.0 copy-start.2
  82.5 0.8 fusion.5
  83.3 0.1 copy-done.21
  83.3 0.2 fusion.19
  83.6 1.0 copy-done.2
  84.6 1.6 convolution_convert_fusion.1
  86.2 0.0 reduce-scatter.3.cloned.1.call-update
  86.2 0.0 reduce-scatter.5.cloned.1.call-start
  86.2 21.4 %reduce-scatter.3.cloned.1.call-done = bf16[32,3584]{1,0:T(8,128)(2,1)} async-done(((bf16[128,3584]{1,0:T(8,128)(2,1)}), bf16[32,3584]{1,0:T(8,128)(2,1)}) %reduce-scatter.3.cloned.1.call-update) | async-done | bytes 229392 | tf_op jit(solution)/shard_map/reduce_scatter | solution.py:157
  107.6 1.1 fusion.25
  108.8 1.3 multiply_reduce_fusion
  110.1 1.2 multiply_convert_fusion
  111.4 0.8 stack.2
  112.2 0.0 copy-start.17
  112.2 91.5 %all_to_all.15 = bf16[32,32,3584]{2,1,0:T(8,128)(2,1)S(1)} all-to-all(bf16[32,32,3584]{2,1,0:T(8,128)(2,1)S(1)} %stack.2), channel_id=1, replica_groups=mesh['req'=32,'mlp'=4] {'req'}, dimensions={0} | all-to-all | bytes 14680064 | tf_op jit(solution)/shard_map/all_to_all | solution.py:169
  203.7 3.0 copy-done.1
  206.7 4.7 %fusion.62 = f32[1024,448]{0,1:T(8,128)} fusion(bf16[1024,3584]{1,0:T(8,128)(2,1)S(1)} %bitcast.81, bf16[3584,448]{0,1:T(8,128)(2,1)S(1)} %copy-done.17), kind=kOutput, calls=%fused_computation.122 | convolution fusion | flops 3288334336 | bytes 12386304 | tf_op jit(solution)/shard_map/dot_general | solution.py:171
  211.5 13.0 %convolution_convert_fusion = bf16[1024,3584]{1,0:T(8,128)(2,1)} fusion(bf16[448,3584]{1,0:T(8,128)(2,1)S(1)} %copy-done, f32[1024,448]{0,1:T(8,128)} %fusion.62, bf16[1024,3584]{1,0:T(8,128)(2,1)} %bitcast.82, bf16[3584,448]{0,1:T(8,128)(2,1)} %param.37), kind=kOutput, calls=%fused_computation.4 | convolution fusion | flops 6584926208 | bytes 22937600 | tf_op jit(solution)/shard_map/dot_general | solution.py:175
  224.5 0.0 reduce-scatter.5.cloned.1.call-update
  224.5 85.2 %reduce-scatter.5.cloned.1.call-done = bf16[32,3584]{1,0:T(8,128)(2,1)} async-done(((bf16[1024,3584]{1,0:T(8,128)(2,1)}), bf16[32,3584]{1,0:T(8,128)(2,1)}) %reduce-scatter.5.cloned.1.call-update) | async-done | bytes 229392 | tf_op jit(solution)/shard_map/reduce_scatter | solution.py:174
  309.7 1.1 fusion.28
  310.9 2.0 fusion.31
  (44 shorter events, 0.1 us)
Async XLA Ops:
  7.2 204.3 %copy-start = (bf16[448,3584]{1,0:T(8,128)(2,1)S(1)}, bf16[448,3584]{1,0:T(8,128)(2,1)}, u32[]{:S(2)}) copy-start(bf16[448,3584]{1,0:T(8,128)(2,1)} %param.38) | copy-start | bytes 9633796
  17.6 8.6 %copy-start.19 = (s32[1,64]{1,0:T(1,128)S(1)}, s32[1,64]{1,0:T(1,128)}, u32[]{:S(2)}) copy-start(s32[1,64]{1,0:T(1,128)} %param.25) | copy-start | bytes 772
  17.6 11.5 %copy-start.11 = (s32[1,128]{1,0:T(1,128)S(1)}, s32[1,128]{1,0:T(1,128)}, u32[]{:S(2)}) copy-start(s32[1,128]{1,0:T(1,128)} %param.23) | copy-start | bytes 1540
  17.6 12.2 %copy-start.13 = (s32[1,4]{1,0:T(1,128)S(1)}, s32[1,4]{1,0:T(1,128)}, u32[]{:S(2)}) copy-start(s32[1,4]{1,0:T(1,128)} %param.24) | copy-start | bytes 52
  17.6 14.6 %copy-start.18 = (f32[3584]{0:T(1024)S(1)}, f32[3584]{0:T(1024)}, u32[]{:S(2)}) copy-start(f32[3584]{0:T(1024)} %param.29) | copy-start | bytes 43012
  17.6 26.0 %all-to-all-start = ((bf16[32,1,64,256]{3,2,1,0:T(8,128)(2,1)}), bf16[32,1,64,256]{3,2,1,0:T(8,128)(2,1)}, u32[]{:S(2)}, u32[]{:S(2)}) async-start(bf16[32,1,64,256]{3,2,1,0:T(8,128)(2,1)} %get-tuple-element.20), calls=%async_computation | async-start | bytes 2097152 | tf_op jit(solution)/shard_map/all_to_all | solution.py:97
  26.7 8.1 %copy-start.16 = (bf16[3584,512]{1,0:T(8,128)(2,1)S(1)}, bf16[3584,512]{1,0:T(8,128)(2,1)}, u32[]{:S(2)}) copy-start(bf16[3584,512]{1,0:T(8,128)(2,1)} %param.30) | copy-start | bytes 11010052
  27.3 7.5 %copy-start.4 = (bf16[128,3584]{1,0:T(8,128)(2,1)S(1)}, bf16[128,3584]{1,0:T(8,128)(2,1)}, u32[]{:S(2)}) copy-start(bf16[128,3584]{1,0:T(8,128)(2,1)} %param.22) | copy-start | bytes 2752516
  29.1 7.1 %copy-start.22 = (f32[128]{0:T(128)}, f32[128]{0:T(128)S(1)}, u32[]{:S(2)}) copy-start(f32[128]{0:T(128)S(1)} %add_rsqrt_fusion.3) | copy-start | bytes 1540
  41.3 9.8 %copy-start.7 = (s32[4096]{0:T(1024)S(1)}, s32[4096]{0:T(1024)}, u32[]{:S(2)}) copy-start(s32[4096]{0:T(1024)} %get-tuple-element.25) | copy-start | bytes 49156
  41.3 9.8 %copy-start.9 = (pred[4096]{0:T(1024)(128)(4,1)S(1)}, pred[4096]{0:T(1024)(128)(4,1)}, u32[]{:S(2)}) copy-start(pred[4096]{0:T(1024)(128)(4,1)} %subtract_compare_fusion) | copy-start | bytes 12292
  41.3 9.8 %copy-start.12 = (s32[1,128]{1,0:T(1,128)S(1)}, s32[1,128]{1,0:T(1,128)}, u32[]{:S(2)}) copy-start(s32[1,128]{1,0:T(1,128)} %param.23) | copy-start | bytes 1540
  41.3 9.8 %copy-start.14 = (s32[128]{0:T(128)S(1)}, s32[128]{0:T(128)}, u32[]{:S(2)}) copy-start(s32[128]{0:T(128)} %get-tuple-element.16) | copy-start | bytes 1540
  43.6 39.7 %copy-start.20 = (bf16[128,256]{1,0:T(8,128)(2,1)}, bf16[128,256]{1,0:T(8,128)(2,1)S(1)}, u32[]{:S(2)}) copy-start(bf16[128,256]{1,0:T(8,128)(2,1)S(1)} %convolution_convert_fusion.2) | copy-start | bytes 196612
  43.6 24.2 %all-to-all-start.1 = ((bf16[32,1,64,256]{3,2,1,0:T(8,128)(2,1)}), bf16[32,1,64,256]{3,2,1,0:T(8,128)(2,1)}, u32[]{:S(2)}, u32[]{:S(2)}) async-start(bf16[32,1,64,256]{3,2,1,0:T(8,128)(2,1)} %get-tuple-element.19), calls=%async_computation.1 | async-start | bytes 2097152 | tf_op jit(solution)/shard_map/all_to_all | solution.py:96
  51.1 56.6 %reduce-scatter.3.cloned.1.call-start = ((), (), s32[]{:S(2)}) async-start(), calls=%async_computation.5 | async-start | bytes 1146880 | tf_op jit(solution)/shard_map/reduce_scatter | solution.py:157
  74.6 3.7 %copy-start.15 = (pred[64]{0:T(512)(128)(4,1)S(1)}, pred[64]{0:T(512)(128)(4,1)}, u32[]{:S(2)}) copy-start(pred[64]{0:T(512)(128)(4,1)} %compare_and_fusion) | copy-start | bytes 196
  78.3 2.7 copy-start.5
  82.4 0.9 copy-start.21
  82.4 2.1 copy-start.2
  84.6 24.2 %copy-start.6 = (f32[3584]{0:T(1024)S(1)}, f32[3584]{0:T(1024)}, u32[]{:S(2)}) copy-start(f32[3584]{0:T(1024)} %param.34) | copy-start | bytes 43012
  84.6 25.5 %copy-start.10 = (f32[3584]{0:T(1024)S(1)}, f32[3584]{0:T(1024)}, u32[]{:S(2)}) copy-start(f32[3584]{0:T(1024)} %param.35) | copy-start | bytes 43012
  86.2 223.6 %reduce-scatter.5.cloned.1.call-start = ((), (), s32[]{:S(2)}) async-start(), calls=%async_computation.6 | async-start | bytes 7569408 | tf_op jit(solution)/shard_map/reduce_scatter | solution.py:174
  112.2 94.6 %copy-start.17 = (bf16[3584,448]{0,1:T(8,128)(2,1)S(1)}, bf16[3584,448]{0,1:T(8,128)(2,1)}, u32[]{:S(2)}) copy-start(bf16[3584,448]{0,1:T(8,128)(2,1)} %param.36) | copy-start | bytes 9633796
  203.7 3.0 copy-start.1
  224.5 86.4 %copy-start.3 = (bf16[32,3584]{1,0:T(8,128)(2,1)S(1)}, bf16[32,3584]{1,0:T(8,128)(2,1)}, u32[]{:S(2)}) copy-start(bf16[32,3584]{1,0:T(8,128)(2,1)} %reduce-scatter.3.cloned.1.call-done) | copy-start | bytes 688132
  224.5 86.4 %copy-start.8 = (f32[3584]{0:T(1024)S(1)}, f32[3584]{0:T(1024)}, u32[]{:S(2)}) copy-start(f32[3584]{0:T(1024)} %param.39) | copy-start | bytes 43012
Sparse Core Ops, SparseCore 0:
  86.3 21.2 reduce-scatter.2
  224.6 85.0 reduce-scatter.4
